TPU v7x, 256 devices: a whole 4x4x8 slice. The times are simulated.
256 devices in a mesh: band: 32 (over x_hi, z, core), var: 8 (over y, x_lo).
Axes of the slice: x: 4 (x_hi: 2, x_lo: 2; x = x_hi * 2 + x_lo), y: 4, z: 8, core: 2. Of those that a mesh axis runs over, the one named last changes fastest.
Arguments:
- patches: bfloat16 [16, 32, 256, 64], P('var', 'band'), may hold values from -6 to 6
- w_embed: bfloat16 [16, 64, 2048], P('var'), may hold values from -0.75 to 0.75
- var_bias: float32 [16, 2048], P('var'), may hold values from -3 to 3
- agg_gain: float32 [2048], replicated, may hold values from 0.1 to 1.9
- wq: bfloat16 [2048, 2048], P(None, 'var'), may hold values from -4 to 4
- wk: bfloat16 [2048, 2048], P(None, 'var'), may hold values from -4 to 4
- wv: bfloat16 [2048, 2048], P(None, 'var'), may hold values from -0.125 to 0.125
- wo: bfloat16 [2048, 2048], P('var'), may hold values from -0.125 to 0.125
- w_up: bfloat16 [2048, 1024], replicated, may hold values from -0.125 to 0.125
- conv1: bfloat16 [9, 64, 64], replicated, may hold values from -0.25 to 0.25
- bias1: float32 [64], replicated, may hold values from -3 to 3
- conv2: bfloat16 [9, 64, 64], replicated, may hold values from -0.25 to 0.25
- cotangent: bfloat16 [128, 64, 1024], P('band', None, 'var'), may hold values from -6 to 6
Outputs:
- field_out: bfloat16 [128, 64, 1024], P('band', None, 'var')
- grad_fine: bfloat16 [128, 64, 1024], P('band', None, 'var')
- grad_conv1: float32 [9, 64, 64], replicated
- grad_conv2: float32 [9, 64, 64], replicated
- grad_bias: float32 [64], replicated
All inputs are finite; a program needn't handle non-finite values.
Results may differ from a plain program's by a relative error of at most 0.03.
Values may be sent and summed in bfloat16 or wider, within the bound.
No kernel may reach another device: no remote copies, remote signals or barrier semaphores. Data moves between devices by JAX's collectives and lax.ppermute only.
A program may use at most 128 MiB of HBM per device.

v0:
```python
import math
import jax
import jax.numpy as jnp
from jax import lax
from jax.sharding import PartitionSpec as P

D = 2048
HD = 128
C = 64
R = 4


def with_halo(cells, sides, width):
    for axis, dim in sides:
        count = lax.axis_size(axis)
        ends = count - 1
        head = lax.slice_in_dim(cells, 0, width, axis=dim)
        tail = lax.slice_in_dim(cells, cells.shape[dim] - width, cells.shape[dim], axis=dim)
        cells = jnp.concatenate(
            [
                lax.ppermute(tail, axis, [(i, (i + 1) % count) for i in range(ends)]),
                cells,
                lax.ppermute(head, axis, [((i + 1) % count, i) for i in range(ends)]),
            ],
            axis=dim,
        )
    return cells


def tap_stack(padded, height, width):
    pieces = [
        padded[row_tap : row_tap + height, :, col_tap : col_tap + width]
        for row_tap in range(3)
        for col_tap in range(3)
    ]
    return jnp.concatenate(pieces, axis=1)


def conv_padded(padded, weight, height, width):
    stacked = tap_stack(padded, height, width)
    return jnp.einsum(
        "ykx,ko->yox",
        stacked,
        weight.reshape(-1, weight.shape[2]),
        preferred_element_type=jnp.float32,
    )


def flipped(weight):
    return jnp.transpose(weight[::-1], (0, 2, 1))


def weight_grad(padded, grads):
    stacked = tap_stack(padded, grads.shape[0], grads.shape[2])
    summed = jnp.einsum("ykx,yox->ko", stacked, grads, preferred_element_type=jnp.float32)
    return summed.reshape(9, padded.shape[1], grads.shape[1])


def normalize(mixed, agg_gain):
    return (
        mixed * lax.rsqrt(jnp.mean(mixed * mixed, axis=-1, keepdims=True) + 1e-05) * agg_gain
    ).astype(jnp.bfloat16)


def gradient_rim(field):
    return with_halo(field, (("band", 0), ("var", 2)), 1)


def on_device(
    patches, w_embed, var_bias, agg_gain, wq, wk, wv, wo, w_up, conv1, bias1, conv2, cotangent
):
    var_count = lax.axis_size("var")
    band_count = lax.axis_size("band")
    var_local, lat_dev, lon_all, patch_len = patches.shape
    lon_dev = lon_all // var_count
    flattened = jnp.transpose(patches, (1, 2, 0, 3)).reshape(
        lat_dev * lon_all, var_local * patch_len
    )
    partial_mix = jnp.dot(
        flattened, w_embed.reshape(var_local * patch_len, D), preferred_element_type=jnp.float32
    )
    partial_mix = (partial_mix + jnp.sum(var_bias, axis=0)).reshape(lat_dev, lon_all, D)
    mixed = lax.psum(partial_mix.astype(jnp.bfloat16), "var").astype(jnp.float32)
    normed_band = normalize(mixed, agg_gain)
    normed_slab = lax.dynamic_slice_in_dim(normed_band, lax.axis_index("var") * lon_dev, lon_dev, 1)
    token_rows = jnp.transpose(
        normed_band.reshape(lat_dev, var_count, lon_dev, D), (1, 0, 2, 3)
    ).reshape(-1, D)
    heads_local = wq.shape[1] // HD
    query_rows = token_rows.shape[0]
    queries = jnp.dot(token_rows, wq, preferred_element_type=jnp.float32).astype(jnp.bfloat16)
    keys_local = jnp.dot(token_rows, wk, preferred_element_type=jnp.float32).astype(jnp.bfloat16)
    values_local = jnp.dot(token_rows, wv, preferred_element_type=jnp.float32).astype(jnp.bfloat16)
    query_heads = queries.reshape(query_rows, heads_local, HD)
    running_max = jnp.full((heads_local, query_rows), -1e30, jnp.float32)
    key_heads = lax.all_gather(keys_local, "band", axis=0, tiled=True).reshape(-1, heads_local, HD)
    value_heads = lax.all_gather(values_local, "band", axis=0, tiled=True).reshape(
        -1, heads_local, HD
    )
    scores = jnp.einsum(
        "qhd,khd->hqk", query_heads, key_heads, preferred_element_type=jnp.float32
    ) / math.sqrt(HD)
    new_max = jnp.maximum(running_max, jnp.max(scores, axis=2))
    weights = jnp.exp(scores - new_max[:, :, None])
    new_sum = jnp.sum(weights, axis=2)
    update = jnp.einsum(
        "hqk,khd->hqd",
        weights.astype(jnp.bfloat16),
        value_heads,
        preferred_element_type=jnp.float32,
    )
    context = (update / new_sum[:, :, None]).astype(jnp.bfloat16)
    context = jnp.transpose(context, (1, 0, 2)).reshape(query_rows, heads_local * HD)
    slab_rows = lat_dev * lon_dev
    attended = lax.psum_scatter(
        jnp.dot(context, wo, preferred_element_type=jnp.float32).astype(jnp.bfloat16),
        "var",
        scatter_dimension=0,
        tiled=True,
    ).astype(jnp.float32)
    hidden = (normed_slab.reshape(slab_rows, D).astype(jnp.float32) + attended).astype(jnp.bfloat16)
    upsampled = jnp.dot(hidden, w_up, preferred_element_type=jnp.float32).astype(jnp.bfloat16)
    height = lat_dev * R
    width = lon_dev * R
    upsampled = jnp.transpose(
        upsampled.reshape(lat_dev, lon_dev, R, R, C), (0, 2, 4, 1, 3)
    ).reshape(height, C, width)
    bias_cols = bias1[None, :, None]
    fine_pad = with_halo(upsampled, (("band", 0), ("var", 2)), 1)
    pre = conv_padded(fine_pad, conv1, height, width) + bias_cols
    active = jax.nn.gelu(pre).astype(jnp.bfloat16)
    active_pad = with_halo(active, (("band", 0), ("var", 2)), 1)
    field_out = (
        conv_padded(active_pad, conv2, height, width) + upsampled.astype(jnp.float32)
    ).astype(jnp.bfloat16)
    cotangent_pad = gradient_rim(cotangent)
    d_active = conv_padded(cotangent_pad, flipped(conv2), height, width)
    d_pre = jax.vjp(jax.nn.gelu, pre)[1](d_active)[0].astype(jnp.bfloat16)
    d_pre_pad = gradient_rim(d_pre)
    grad_fine = (
        cotangent.astype(jnp.float32) + conv_padded(d_pre_pad, flipped(conv1), height, width)
    ).astype(jnp.bfloat16)
    factor = 1.0 / math.sqrt(height * band_count * width * var_count)
    first_terms = weight_grad(fine_pad, d_pre) * factor
    second_terms = weight_grad(active_pad, cotangent) * factor
    bias_terms = jnp.sum(d_pre.astype(jnp.float32), axis=(0, 2)) * factor
    grad_conv1, grad_conv2, grad_bias = lax.psum(
        (first_terms, second_terms, bias_terms), ("band", "var")
    )
    return (field_out, grad_fine, grad_conv1, grad_conv2, grad_bias)


def solution(mesh):
    in_specs = (
        P("var", "band", None, None),
        P("var", None, None),
        P("var", None),
        P(),
        P(None, "var"),
        P(None, "var"),
        P(None, "var"),
        P("var", None),
        P(),
        P(),
        P(),
        P(),
        P("band", None, "var"),
    )
    out_specs = (P("band", None, "var"), P("band", None, "var"), P(), P(), P())
    return jax.shard_map(
        on_device, mesh=mesh, in_specs=in_specs, out_specs=out_specs, check_vma=False
    )
```

profile of v0, /device:TPU:1, one launch (start us, length us, event | category | flops | bytes accessed | tf_op | source)
XLA Modules:
  0.0 733.0 jit_solution(12546269796696864949)
XLA Ops:
  8.1 2.5 fusion.10
  10.7 85.5 %all-reduce.4.cloned.1.call-done = bf16[1,256,2048]{2,1,0:T(8,128)(2,1)} async-done(((bf16[1,256,2048]{2,1,0:T(8,128)(2,1)}), bf16[1,256,2048]{2,1,0:T(8,128)(2,1)}) %all-reduce.4.cloned.1.call-update) | async-done | bytes 1048592 | tf_op jit(solution)/shard_map/psum | solution.py:83
  100.4 2.3 convolution_convert_fusion.1
  102.8 1.7 convolution_convert_fusion.3
  104.6 86.7 %all-gather.3.cloned.1.call-done = bf16[8192,256]{1,0:T(8,128)(2,1)} async-done(((bf16[256,256]{1,0:T(8,128)(2,1)}), bf16[8192,256]{1,0:T(8,128)(2,1)}) %all-gather.3.cloned.1.call-update) | async-done | bytes 4194320 | tf_op jit(solution)/shard_map/all_gather | solution.py:96
  191.3 9.3 %multiply_reduce_fusion = (f32[2,256]{1,0:T(2,128)S(1)}, f32[2,256,8192]{2,1,0:T(8,128)}) fusion(bf16[256,2,128]{0,2,1:T(8,128)(2,1)S(1)} %bitcast.117, bf16[8192,256]{1,0:T(8,128)(2,1)} %all-gather.3.cloned.1.call-done), kind=kOutput, calls=%fused_computation.1 | convolution fusion | flops 1082129920 | bytes 21104640 | tf_op jit(solution)/shard_map/qhd,khd->hqk/dot_general | solution.py:100
  200.6 8.8 %fusion = f32[2,256]{1,0:T(2,128)S(1)} fusion(f32[2,256,8192]{2,1,0:T(8,128)} %get-tuple-element.32, f32[2,256]{1,0:T(2,128)S(1)} %broadcast_maximum_fusion), kind=kLoop, calls=%fused_computation.2 | loop fusion | flops 12582400 | bytes 16781312 | tf_op jit(solution)/shard_map/reduce_sum | solution.py:105
  209.4 68.6 %all-gather.5.cloned.1.call-done = bf16[8192,256]{1,0:T(8,128)(2,1)} async-done(((bf16[256,256]{1,0:T(8,128)(2,1)}), bf16[8192,256]{1,0:T(8,128)(2,1)}) %all-gather.5.cloned.1.call-update) | async-done | bytes 4194320 | tf_op jit(solution)/shard_map/all_gather | solution.py:97
  278.0 6.4 copy.52
  284.4 10.4 %fusion.27 = bf16[256,2,128]{0,2,1:T(8,128)(2,1)S(1)} fusion(bf16[8192,2,128]{0,2,1:T(8,128)(2,1)} %bitcast.110, f32[2,256,8192]{2,1,0:T(8,128)} %get-tuple-element.32, f32[2,256]{1,0:T(2,128)S(1)} %broadcast_maximum_fusion, f32[256,2]{0,1:T(2,128)S(1)} %bitcast.125), kind=kOutput, calls=%fused_computation.38 | convolution fusion | flops 1086455808 | bytes 21106688 | tf_op jit(solution)/shard_map/hqk,khd->hqd/dot_general | solution.py:106
  296.4 3.0 collective-permute-start.8
  299.4 1.9 collective-permute-start.9
  301.5 3.0 collective-permute-done.9
  304.6 2.2 collective-permute-start.10
  311.0 6.8 collective-permute-done.11
  321.3 11.4 %reduce-scatter.2.cloned.1.call-done = bf16[32,2048]{1,0:T(8,128)(2,1)} async-done(((bf16[256,2048]{1,0:T(8,128)(2,1)}), bf16[32,2048]{1,0:T(8,128)(2,1)}) %reduce-scatter.2.cloned.1.call-update) | async-done | bytes 131088 | tf_op jit(solution)/shard_map/reduce_scatter | solution.py:115
  332.7 3.1 convolution_convert_fusion.4
  336.1 8.2 %collective-permute-start = (bf16[1,64,128]{2,1,0:T(8,128)(2,1)S(1)}, bf16[1,64,128]{2,1,0:T(8,128)(2,1)S(1)}, u32[]{:S(2)}, u32[]{:S(2)}) collective-permute-start(bf16[1,64,128]{2,1,0:T(8,128)(2,1)S(1)} %copy.32), channel_id=1, source_target_pairs={{0,8},{8,16},{16,24},{24,32},{32,40},{40,48},{48,56},{56,64},{64,7... | collective-permute-start | bytes 49160 | tf_op jit(solution)/shard_map/ppermute | solution.py:21
  344.4 1.9 collective-permute-start.1
  347.1 2.4 collective-permute-done.1
  349.6 1.6 collective-permute-start.2
  353.2 3.3 collective-permute-done.3
  360.2 3.7 collective-permute-start.4
  363.8 1.9 collective-permute-start.5
  365.8 3.6 collective-permute-start.12
  369.4 1.9 collective-permute-start.13
  371.4 84.9 %psum.31 = f32[64]{0:T(128)} all-reduce(f32[64]{0:T(128)S(1)} %broadcast_multiply_fusion), channel_id=1, replica_groups=mesh['band'=32,'var'=8] {'band','var'}, use_global_device_ids=true, to_apply=%region_9.0 | all-reduce | flops 64 | bytes 512 | tf_op jit(solution)/shard_map/psum | solution.py:147
  459.1 4.0 collective-permute-start.14
  466.2 4.2 collective-permute-done.15
  472.8 250.3 %all-reduce.6.cloned.1.call-done = (f32[9,64,64]{2,1,0:T(8,128)}, f32[9,64,64]{2,1,0:T(8,128)}) async-done(((f32[9,64,64]{2,1,0:T(8,128)}, f32[9,64,64]{2,1,0:T(8,128)}), (f32[9,64,64]{2,1,0:T(8,128)}, f32[9,64,64]{2,1,0:T(8,128)})) %all-reduce.6.cloned.1.call-update) | async-done | bytes 294928 | tf_op jit(solution)/shard_map/psum | solution.py:147
  723.1 1.7 copy.104
  724.7 1.7 copy.105
  (118 shorter events, 29.6 us)
Async XLA Ops:
  7.2 287.6 %copy-start = (bf16[256,2048]{1,0:T(8,128)(2,1)S(1)}, bf16[256,2048]{1,0:T(8,128)(2,1)}, u32[]{:S(2)}) copy-start(bf16[256,2048]{1,0:T(8,128)(2,1)} %param.20) | copy-start | bytes 3145732
  7.2 92.1 %copy-start.2 = (bf16[2048,256]{1,0:T(8,128)(2,1)S(1)}, bf16[2048,256]{1,0:T(8,128)(2,1)}, u32[]{:S(2)}) copy-start(bf16[2048,256]{1,0:T(8,128)(2,1)} %param.18) | copy-start | bytes 3145732
  7.2 89.0 %all-reduce.4.cloned.1.call-start = ((), (), s32[]{:S(2)}) async-start(), calls=%async_computation.1 | async-start | bytes 2097152 | tf_op jit(solution)/shard_map/psum | solution.py:83
  10.6 180.7 %all-gather.3.cloned.1.call-start = ((), (), s32[]{:S(2)}) async-start(), calls=%async_computation.2 | async-start | bytes 4325376 | tf_op jit(solution)/shard_map/all_gather | solution.py:96
  100.4 177.6 %all-gather.5.cloned.1.call-start = ((), (), s32[]{:S(2)}) async-start(), calls=%async_computation.3 | async-start | bytes 4325376 | tf_op jit(solution)/shard_map/all_gather | solution.py:97
  102.8 229.9 %reduce-scatter.2.cloned.1.call-start = ((), (), s32[]{:S(2)}) async-start(), calls=%async_computation.4 | async-start | bytes 1179648 | tf_op jit(solution)/shard_map/reduce_scatter | solution.py:115
  284.4 12.0 %copy-start.1 = (bf16[4,64,128]{2,1,0:T(8,128)(2,1)S(1)}, bf16[4,64,128]{2,1,0:T(8,128)(2,1)}, u32[]{:S(2)}) copy-start(bf16[4,64,128]{2,1,0:T(8,128)(2,1)} %param.25) | copy-start | bytes 196612
  284.4 17.0 %copy-start.3 = (bf16[9,64,64]{2,1,0:T(8,128)(2,1)S(1)}, bf16[9,64,64]{2,1,0:T(8,128)(2,1)}, u32[]{:S(2)}) copy-start(bf16[9,64,64]{2,1,0:T(8,128)(2,1)} %param.24) | copy-start | bytes 221188
  284.4 17.0 %copy-start.4 = (bf16[9,64,64]{2,1,0:T(8,128)(2,1)S(1)}, bf16[9,64,64]{2,1,0:T(8,128)(2,1)}, u32[]{:S(2)}) copy-start(bf16[9,64,64]{2,1,0:T(8,128)(2,1)} %param.22) | copy-start | bytes 221188
  296.3 426.7 %all-reduce.6.cloned.1.call-start = ((), (), s32[]{:S(2)}) async-start(), calls=%async_computation.5 | async-start | bytes 1179648 | tf_op jit(solution)/shard_map/psum | solution.py:147
  296.4 5.0 collective-permute-start.8
  299.4 5.1 collective-permute-start.9
  301.4 3.1 copy-start.5
  304.6 4.3 collective-permute-start.10
  307.1 10.6 %collective-permute-start.11 = (bf16[6,64,1]{2,1,0:T(8,128)(2,1)S(1)}, bf16[6,64,1]{2,1,0:T(8,128)(2,1)S(1)}, u32[]{:S(2)}, u32[]{:S(2)}) collective-permute-start(bf16[6,64,1]{2,1,0:T(8,128)(2,1)S(1)} %get-tuple-element.15), channel_id=1, source_target_pairs={{1,0},{2,1},{3,2},{4,3},{5,4},{6,5},{7,6},{9,8},{10,9},{11,10},{12... | collective-permute-start | bytes 2312 | tf_op jit(solution)/shard_map/ppermute | solution.py:23
  321.3 35.8 %copy-start.6 = (f32[64]{0:T(128)S(1)}, f32[64]{0:T(128)}, u32[]{:S(2)}) copy-start(f32[64]{0:T(128)} %param.23) | copy-start | bytes 772
  336.1 11.0 %collective-permute-start = (bf16[1,64,128]{2,1,0:T(8,128)(2,1)S(1)}, bf16[1,64,128]{2,1,0:T(8,128)(2,1)S(1)}, u32[]{:S(2)}, u32[]{:S(2)}) collective-permute-start(bf16[1,64,128]{2,1,0:T(8,128)(2,1)S(1)} %copy.32), channel_id=1, source_target_pairs={{0,8},{8,16},{16,24},{24,32},{32,40},{40,48},{48,56},{56,64},{64,7... | collective-permute-start | bytes 49160 | tf_op jit(solution)/shard_map/ppermute | solution.py:21
  344.4 5.1 collective-permute-start.1
  349.6 3.6 collective-permute-start.2
  351.2 5.4 collective-permute-start.3
  360.2 96.1 %collective-permute-start.4 = (bf16[1,64,128]{2,1,0:T(8,128)(2,1)S(1)}, bf16[1,64,128]{2,1,0:T(8,128)(2,1)S(1)}, u32[]{:S(2)}, u32[]{:S(2)}) collective-permute-start(bf16[1,64,128]{2,1,0:T(8,128)(2,1)S(1)} %get-tuple-element.29), channel_id=1, source_target_pairs={{0,8},{8,16},{16,24},{24,32},{32,40},{40,48},{48,56},{56,64},{64,7... | collective-permute-start | bytes 49160 | tf_op jit(solution)/shard_map/ppermute | solution.py:21
  363.8 92.4 %collective-permute-start.5 = (bf16[1,64,128]{2,1,0:T(8,128)(2,1)S(1)}, bf16[1,64,128]{2,1,0:T(8,128)(2,1)S(1)}, u32[]{:S(2)}, u32[]{:S(2)}) collective-permute-start(bf16[1,64,128]{2,1,0:T(8,128)(2,1)S(1)} %get-tuple-element.30), channel_id=1, source_target_pairs={{8,0},{16,8},{24,16},{32,24},{40,32},{48,40},{56,48},{64,56},{72,6... | collective-permute-start | bytes 49160 | tf_op jit(solution)/shard_map/ppermute | solution.py:23
  365.8 93.2 %collective-permute-start.12 = (bf16[1,64,128]{2,1,0:T(8,128)(2,1)S(1)}, bf16[1,64,128]{2,1,0:T(8,128)(2,1)S(1)}, u32[]{:S(2)}, u32[]{:S(2)}) collective-permute-start(bf16[1,64,128]{2,1,0:T(8,128)(2,1)S(1)} %get-tuple-element.25), channel_id=1, source_target_pairs={{0,8},{8,16},{16,24},{24,32},{32,40},{40,48},{48,56},{56,64},{64,7... | collective-permute-start | bytes 49160 | tf_op jit(solution)/shard_map/ppermute | solution.py:21
  369.4 89.6 %collective-permute-start.13 = (bf16[1,64,128]{2,1,0:T(8,128)(2,1)S(1)}, bf16[1,64,128]{2,1,0:T(8,128)(2,1)S(1)}, u32[]{:S(2)}, u32[]{:S(2)}) collective-permute-start(bf16[1,64,128]{2,1,0:T(8,128)(2,1)S(1)} %get-tuple-element.26), channel_id=1, source_target_pairs={{8,0},{16,8},{24,16},{32,24},{40,32},{48,40},{56,48},{64,56},{72,6... | collective-permute-start | bytes 49160 | tf_op jit(solution)/shard_map/ppermute | solution.py:23
  456.4 8.1 %collective-permute-start.6 = (bf16[6,64,1]{2,1,0:T(8,128)(2,1)S(1)}, bf16[6,64,1]{2,1,0:T(8,128)(2,1)S(1)}, u32[]{:S(2)}, u32[]{:S(2)}) collective-permute-start(bf16[6,64,1]{2,1,0:T(8,128)(2,1)S(1)} %get-tuple-element.20), channel_id=1, source_target_pairs={{0,1},{1,2},{2,3},{3,4},{4,5},{5,6},{6,7},{8,9},{9,10},{10,11},{11... | collective-permute-start | bytes 2312 | tf_op jit(solution)/shard_map/ppermute | solution.py:21
  457.7 6.8 collective-permute-start.7
  459.1 7.1 collective-permute-start.14
  463.1 7.3 collective-permute-start.15
Sparse Core Ops, SparseCore 0:
  10.8 85.3 all-reduce.3
  100.5 90.7 all-gather.2
  194.7 83.2 all-gather.4
  296.4 36.2 reduce-scatter.1
  472.0 250.9 all-reduce.5
where the time goes:
time: 734 us; the launch traced here: 733 us
  waiting for transfers between devices  523 us (71%)
  blocking collectives  84.9 us (12%)
  starting transfers between devices  40.9 us (6%)
  matrix products  36.1 us (5%)
  other arithmetic  19.6 us (3%)
  local copies, waits for them, and re-layouts  14.5 us (2%)
  between operations  14.4 us (2%)
    psum x1, waiting for transfers between devices, on_device(): lax.psum((first_terms, second_terms, bias_terms), ('band', 'var'))  250 us
    all_gather x1, waiting for transfers between devices, on_device(): lax.all_gather(keys_local, 'band', axis=0, tiled=True)  86.7 us
    psum x1, waiting for transfers between devices, on_device(): lax.psum(partial_mix.astype(jnp.bfloat16), 'var').astype(jnp.float32)  85.5 us
    psum x1, blocking collectives, on_device(): lax.psum((first_terms, second_terms, bias_terms), ('band', 'var'))  84.9 us
    all_gather x1, waiting for transfers between devices, on_device(): lax.all_gather(values_local, 'band', axis=0, tiled=True)  68.6 us
    ppermute x8, starting transfers between devices, with_halo(): lax.ppermute(tail, axis, [(i, (i + 1) % count) for i in range(ends)])  27.6 us
    ppermute x8, waiting for transfers between devices, with_halo(): lax.ppermute(head, axis, [((i + 1) % count, i) for i in range(ends)])  19.7 us
  transfers between devices with their start and end apart: 21, of which 11 were waited for; matrix products, arithmetic and copies ran while one was open for 4% of the time, Pallas kernels for 0%

commit v1 on v0

--- a/solution.py
+++ b/solution.py
@@ -8,6 +8,13 @@
 HD = 128
 C = 64
 R = 4
+
+
+def all_by_exchange(array, axis, dim):
+    peers = lax.axis_size(axis)
+    blocks = jnp.stack([array for _ in range(peers)])
+    blocks = lax.all_to_all(blocks, axis, split_axis=0, concat_axis=0)
+    return jnp.concatenate(blocks, axis=dim)
 
 
 def with_halo(cells, sides, width):
@@ -93,7 +100,7 @@
     values_local = jnp.dot(token_rows, wv, preferred_element_type=jnp.float32).astype(jnp.bfloat16)
     query_heads = queries.reshape(query_rows, heads_local, HD)
     running_max = jnp.full((heads_local, query_rows), -1e30, jnp.float32)
-    key_heads = lax.all_gather(keys_local, "band", axis=0, tiled=True).reshape(-1, heads_local, HD)
+    key_heads = all_by_exchange(keys_local, "band", 0).reshape(-1, heads_local, HD)
     value_heads = lax.all_gather(values_local, "band", axis=0, tiled=True).reshape(
         -1, heads_local, HD
     )

time: 734 us -> 713 us (0.971)
  waiting for transfers between devices: 523 us -> 468 us
  starting transfers between devices: 40.9 us -> 58.4 us
  local copies, waits for them, and re-layouts: 14.5 us -> 31.2 us
    all_to_all x0 -> x1, waiting for transfers between devices: none -> 105 us  [all_by_exchange(): blocks = lax.all_to_all(blocks, axis, split_axis=0, concat_axis=0)]
    all_gather x1 -> x0, waiting for transfers between devices: 86.7 us -> none  [on_device(): lax.all_gather(keys_local, 'band', axis=0, tiled=True)]
    all_gather x1, waiting for transfers between devices: 68.6 us -> 0.02 us  [on_device(): lax.all_gather(values_local, 'band', axis=0, tiled=True)]
    all_to_all x0 -> x1, starting transfers between devices: none -> 14.3 us  [all_by_exchange(): blocks = lax.all_to_all(blocks, axis, split_axis=0, concat_axis=0)]
    another operation x0 -> x2, local copies, waits for them, and re-layouts: none -> 9.93 us  [the longest x1 7.44 us: on_device(): all_by_exchange(keys_local, 'band', 0).reshape(-1, heads_local, HD)]
  transfers between devices with their start and end apart: 21 -> 21, of which waited for: 11 -> 10; matrix products, arithmetic and copies ran while one was open for 4% -> 7% of each run, Pallas kernels for 0% -> 0%
where the time goes in v1:
time: 713 us; the launch traced here: 711 us
  waiting for transfers between devices  468 us (66%)
  blocking collectives  84.1 us (12%)
  starting transfers between devices  58.4 us (8%)
  matrix products  35.3 us (5%)
  local copies, waits for them, and re-layouts  31.2 us (4%)
  other arithmetic  19.4 us (3%)
  between operations  14.4 us (2%)
    psum x1, waiting for transfers between devices, on_device(): lax.psum((first_terms, second_terms, bias_terms), ('band', 'var'))  250 us
    all_to_all x1, waiting for transfers between devices, all_by_exchange(): blocks = lax.all_to_all(blocks, axis, split_axis=0, concat_axis=0)  105 us
    psum x1, waiting for transfers between devices, on_device(): lax.psum(partial_mix.astype(jnp.bfloat16), 'var').astype(jnp.float32)  85.5 us
    psum x1, blocking collectives, on_device(): lax.psum((first_terms, second_terms, bias_terms), ('band', 'var'))  84.1 us
    ppermute x8, starting transfers between devices, with_halo(): lax.ppermute(tail, axis, [(i, (i + 1) % count) for i in range(ends)])  30.8 us
    ppermute x8, waiting for transfers between devices, with_halo(): lax.ppermute(head, axis, [((i + 1) % count, i) for i in range(ends)])  15.2 us
    all_to_all x1, starting transfers between devices, all_by_exchange(): blocks = lax.all_to_all(blocks, axis, split_axis=0, concat_axis=0)  14.3 us
  transfers between devices with their start and end apart: 21, of which 10 were waited for; matrix products, arithmetic and copies ran while one was open for 7% of the time, Pallas kernels for 0%

profile of v1, /device:TPU:1, one launch (start us, length us, event | category | flops | bytes accessed | tf_op | source)
XLA Modules:
  0.0 711.4 jit_solution(4450462033718046084)
XLA Ops:
  8.1 2.5 fusion.7
  10.6 85.5 %all-reduce.4.cloned.1.call-done = bf16[1,256,2048]{2,1,0:T(8,128)(2,1)} async-done(((bf16[1,256,2048]{2,1,0:T(8,128)(2,1)}), bf16[1,256,2048]{2,1,0:T(8,128)(2,1)}) %all-reduce.4.cloned.1.call-update) | async-done | bytes 1048592 | tf_op jit(solution)/shard_map/psum | solution.py:90
  99.8 2.5 stack.2
  102.3 14.3 %all-to-all-start = ((bf16[32,256,256]{1,2,0:T(8,128)(2,1)}), bf16[32,256,256]{1,2,0:T(8,128)(2,1)}, u32[]{:S(2)}, u32[]{:S(2)}) async-start(bf16[32,256,256]{1,2,0:T(8,128)(2,1)} %stack.2), calls=%async_computation | async-start | bytes 8388608 | tf_op jit(solution)/shard_map/all_to_all | solution.py:16
  117.8 1.7 convolution_convert_fusion.3
  119.6 104.7 %all-to-all-done = bf16[32,256,256]{1,2,0:T(8,128)(2,1)} async-done(((bf16[32,256,256]{1,2,0:T(8,128)(2,1)}), bf16[32,256,256]{1,2,0:T(8,128)(2,1)}, u32[]{:S(2)}, u32[]{:S(2)}) %all-to-all-start) | async-done | bytes 4194336 | tf_op jit(solution)/shard_map/all_to_all | solution.py:16
  224.3 6.6 copy.48
  230.9 7.4 %reshape_reshape.3 = bf16[8192,2,128]{0,2,1:T(8,128)(2,1)} reshape(bf16[32,256,256]{1,0,2:T(8,128)(2,1)} %copy.48) | data formatting | bytes 8388608 | tf_op jit(solution)/shard_map/reshape;reshape | solution.py:103
  238.3 10.4 %multiply_reduce_fusion = (f32[2,256]{1,0:T(2,128)S(1)}, f32[2,256,8192]{2,1,0:T(8,128)}) fusion(bf16[256,2,128]{0,2,1:T(8,128)(2,1)S(1)} %bitcast.111, bf16[8192,2,128]{0,2,1:T(8,128)(2,1)} %reshape_reshape.3), kind=kOutput, calls=%fused_computation.1 | convolution fusion | flops 1082129920 | bytes 21104640 | tf_op jit(solution)/shard_map/qhd,khd->hqk/dot_general | solution.py:107
  248.7 8.6 %fusion = f32[2,256]{1,0:T(2,128)S(1)} fusion(f32[2,256,8192]{2,1,0:T(8,128)} %get-tuple-element.32, f32[2,256]{1,0:T(2,128)S(1)} %broadcast_maximum_fusion), kind=kLoop, calls=%fused_computation.2 | loop fusion | flops 12582400 | bytes 16781312 | tf_op jit(solution)/shard_map/reduce_sum | solution.py:112
  257.3 6.4 copy.74
  263.7 10.4 %fusion.24 = bf16[256,2,128]{0,2,1:T(8,128)(2,1)S(1)} fusion(bf16[8192,2,128]{0,2,1:T(8,128)(2,1)} %bitcast.104, f32[2,256,8192]{2,1,0:T(8,128)} %get-tuple-element.32, f32[2,256]{1,0:T(2,128)S(1)} %broadcast_maximum_fusion, f32[256,2]{0,1:T(2,128)S(1)} %bitcast.119), kind=kOutput, calls=%fused_computation.35 | convolution fusion | flops 1086455808 | bytes 21106688 | tf_op jit(solution)/shard_map/hqk,khd->hqd/dot_general | solution.py:113
  275.7 6.6 collective-permute-start.8
  282.3 1.9 collective-permute-start.9
  284.3 3.4 collective-permute-done.9
  290.8 1.9 collective-permute-done.10
  294.7 2.2 collective-permute-done.11
  300.5 11.0 %reduce-scatter.2.cloned.1.call-done = bf16[32,2048]{1,0:T(8,128)(2,1)} async-done(((bf16[256,2048]{1,0:T(8,128)(2,1)}), bf16[32,2048]{1,0:T(8,128)(2,1)}) %reduce-scatter.2.cloned.1.call-update) | async-done | bytes 131088 | tf_op jit(solution)/shard_map/reduce_scatter | solution.py:122
  311.5 3.1 convolution_convert_fusion.4
  314.9 8.6 %collective-permute-start = (bf16[1,64,128]{2,1,0:T(8,128)(2,1)S(1)}, bf16[1,64,128]{2,1,0:T(8,128)(2,1)S(1)}, u32[]{:S(2)}, u32[]{:S(2)}) collective-permute-start(bf16[1,64,128]{2,1,0:T(8,128)(2,1)S(1)} %copy.53), channel_id=1, source_target_pairs={{0,8},{8,16},{16,24},{24,32},{32,40},{40,48},{48,56},{56,64},{64,7... | collective-permute-start | bytes 49160 | tf_op jit(solution)/shard_map/ppermute | solution.py:28
  323.6 1.9 collective-permute-start.1
  326.3 2.4 collective-permute-done.1
  332.3 3.1 collective-permute-done.3
  339.0 3.9 collective-permute-start.4
  343.0 1.9 collective-permute-start.5
  344.9 3.6 collective-permute-start.12
  348.5 1.9 collective-permute-start.13
  350.5 84.1 %psum.31 = f32[64]{0:T(128)} all-reduce(f32[64]{0:T(128)S(1)} %broadcast_multiply_fusion), channel_id=1, replica_groups=mesh['band'=32,'var'=8] {'band','var'}, use_global_device_ids=true, to_apply=%region_9.0 | all-reduce | flops 64 | bytes 512 | tf_op jit(solution)/shard_map/psum | solution.py:154
  437.8 4.0 collective-permute-start.14
  444.8 4.0 collective-permute-done.15
  451.3 250.1 %all-reduce.6.cloned.1.call-done = (f32[9,64,64]{2,1,0:T(8,128)}, f32[9,64,64]{2,1,0:T(8,128)}) async-done(((f32[9,64,64]{2,1,0:T(8,128)}, f32[9,64,64]{2,1,0:T(8,128)}), (f32[9,64,64]{2,1,0:T(8,128)}, f32[9,64,64]{2,1,0:T(8,128)})) %all-reduce.6.cloned.1.call-update) | async-done | bytes 294928 | tf_op jit(solution)/shard_map/psum | solution.py:154
  701.5 1.7 copy.119
  (123 shorter events, 34.5 us)
Async XLA Ops:
  7.2 267.0 %copy-start = (bf16[256,2048]{1,0:T(8,128)(2,1)S(1)}, bf16[256,2048]{1,0:T(8,128)(2,1)}, u32[]{:S(2)}) copy-start(bf16[256,2048]{1,0:T(8,128)(2,1)} %param.20) | copy-start | bytes 3145732
  7.2 92.1 %copy-start.2 = (bf16[2048,256]{1,0:T(8,128)(2,1)S(1)}, bf16[2048,256]{1,0:T(8,128)(2,1)}, u32[]{:S(2)}) copy-start(bf16[2048,256]{1,0:T(8,128)(2,1)} %param.18) | copy-start | bytes 3145732
  7.2 89.0 %all-reduce.4.cloned.1.call-start = ((), (), s32[]{:S(2)}) async-start(), calls=%async_computation.2 | async-start | bytes 2097152 | tf_op jit(solution)/shard_map/psum | solution.py:90
  102.3 14.4 %copy-start.3 = (bf16[2048,256]{1,0:T(8,128)(2,1)S(1)}, bf16[2048,256]{1,0:T(8,128)(2,1)}, u32[]{:S(2)}) copy-start(bf16[2048,256]{1,0:T(8,128)(2,1)} %param.19) | copy-start | bytes 3145732
  102.3 122.0 %all-to-all-start = ((bf16[32,256,256]{1,2,0:T(8,128)(2,1)}), bf16[32,256,256]{1,2,0:T(8,128)(2,1)}, u32[]{:S(2)}, u32[]{:S(2)}) async-start(bf16[32,256,256]{1,2,0:T(8,128)(2,1)} %stack.2), calls=%async_computation | async-start | bytes 8388608 | tf_op jit(solution)/shard_map/all_to_all | solution.py:16
  116.6 140.7 %all-gather.2.cloned.1.call-start = ((), (), s32[]{:S(2)}) async-start(), calls=%async_computation.3 | async-start | bytes 4325376 | tf_op jit(solution)/shard_map/all_gather | solution.py:104
  117.8 193.7 %reduce-scatter.2.cloned.1.call-start = ((), (), s32[]{:S(2)}) async-start(), calls=%async_computation.4 | async-start | bytes 1179648 | tf_op jit(solution)/shard_map/reduce_scatter | solution.py:122
  263.7 12.0 %copy-start.1 = (bf16[4,64,128]{2,1,0:T(8,128)(2,1)S(1)}, bf16[4,64,128]{2,1,0:T(8,128)(2,1)}, u32[]{:S(2)}) copy-start(bf16[4,64,128]{2,1,0:T(8,128)(2,1)} %param.25) | copy-start | bytes 196612
  263.7 20.5 %copy-start.4 = (bf16[9,64,64]{2,1,0:T(8,128)(2,1)S(1)}, bf16[9,64,64]{2,1,0:T(8,128)(2,1)}, u32[]{:S(2)}) copy-start(bf16[9,64,64]{2,1,0:T(8,128)(2,1)} %param.24) | copy-start | bytes 221188
  263.7 20.6 %copy-start.5 = (bf16[9,64,64]{2,1,0:T(8,128)(2,1)S(1)}, bf16[9,64,64]{2,1,0:T(8,128)(2,1)}, u32[]{:S(2)}) copy-start(bf16[9,64,64]{2,1,0:T(8,128)(2,1)} %param.22) | copy-start | bytes 221188
  275.6 425.8 %all-reduce.6.cloned.1.call-start = ((), (), s32[]{:S(2)}) async-start(), calls=%async_computation.5 | async-start | bytes 1179648 | tf_op jit(solution)/shard_map/psum | solution.py:154
  275.7 8.6 %collective-permute-start.8 = (bf16[1,64,128]{2,1,0:T(8,128)(2,1)S(1)}, bf16[1,64,128]{2,1,0:T(8,128)(2,1)S(1)}, u32[]{:S(2)}, u32[]{:S(2)}) collective-permute-start(bf16[1,64,128]{2,1,0:T(8,128)(2,1)S(1)} %get-tuple-element.28), channel_id=1, source_target_pairs={{0,8},{8,16},{16,24},{24,32},{32,40},{40,48},{48,56},{56,64},{64,7... | collective-permute-start | bytes 49160 | tf_op jit(solution)/shard_map/ppermute | solution.py:28
  282.3 5.5 collective-permute-start.9
  284.3 3.5 copy-start.6
  287.9 4.8 collective-permute-start.10
  289.5 7.5 %collective-permute-start.11 = (bf16[6,64,1]{2,1,0:T(8,128)(2,1)S(1)}, bf16[6,64,1]{2,1,0:T(8,128)(2,1)S(1)}, u32[]{:S(2)}, u32[]{:S(2)}) collective-permute-start(bf16[6,64,1]{2,1,0:T(8,128)(2,1)S(1)} %get-tuple-element.15), channel_id=1, source_target_pairs={{1,0},{2,1},{3,2},{4,3},{5,4},{6,5},{7,6},{9,8},{10,9},{11,10},{12... | collective-permute-start | bytes 2312 | tf_op jit(solution)/shard_map/ppermute | solution.py:30
  300.5 35.5 %copy-start.7 = (f32[64]{0:T(128)S(1)}, f32[64]{0:T(128)}, u32[]{:S(2)}) copy-start(f32[64]{0:T(128)} %param.23) | copy-start | bytes 772
  314.9 11.3 %collective-permute-start = (bf16[1,64,128]{2,1,0:T(8,128)(2,1)S(1)}, bf16[1,64,128]{2,1,0:T(8,128)(2,1)S(1)}, u32[]{:S(2)}, u32[]{:S(2)}) collective-permute-start(bf16[1,64,128]{2,1,0:T(8,128)(2,1)S(1)} %copy.53), channel_id=1, source_target_pairs={{0,8},{8,16},{16,24},{24,32},{32,40},{40,48},{48,56},{56,64},{64,7... | collective-permute-start | bytes 49160 | tf_op jit(solution)/shard_map/ppermute | solution.py:28
  323.6 5.1 collective-permute-start.1
  328.8 3.6 collective-permute-start.2
  330.1 5.4 collective-permute-start.3
  339.0 95.6 %collective-permute-start.4 = (bf16[1,64,128]{2,1,0:T(8,128)(2,1)S(1)}, bf16[1,64,128]{2,1,0:T(8,128)(2,1)S(1)}, u32[]{:S(2)}, u32[]{:S(2)}) collective-permute-start(bf16[1,64,128]{2,1,0:T(8,128)(2,1)S(1)} %get-tuple-element.29), channel_id=1, source_target_pairs={{0,8},{8,16},{16,24},{24,32},{32,40},{40,48},{48,56},{56,64},{64,7... | collective-permute-start | bytes 49160 | tf_op jit(solution)/shard_map/ppermute | solution.py:28
  343.0 91.7 %collective-permute-start.5 = (bf16[1,64,128]{2,1,0:T(8,128)(2,1)S(1)}, bf16[1,64,128]{2,1,0:T(8,128)(2,1)S(1)}, u32[]{:S(2)}, u32[]{:S(2)}) collective-permute-start(bf16[1,64,128]{2,1,0:T(8,128)(2,1)S(1)} %get-tuple-element.30), channel_id=1, source_target_pairs={{8,0},{16,8},{24,16},{32,24},{40,32},{48,40},{56,48},{64,56},{72,6... | collective-permute-start | bytes 49160 | tf_op jit(solution)/shard_map/ppermute | solution.py:30
  344.9 92.7 %collective-permute-start.12 = (bf16[1,64,128]{2,1,0:T(8,128)(2,1)S(1)}, bf16[1,64,128]{2,1,0:T(8,128)(2,1)S(1)}, u32[]{:S(2)}, u32[]{:S(2)}) collective-permute-start(bf16[1,64,128]{2,1,0:T(8,128)(2,1)S(1)} %get-tuple-element.25), channel_id=1, source_target_pairs={{0,8},{8,16},{16,24},{24,32},{32,40},{40,48},{48,56},{56,64},{64,7... | collective-permute-start | bytes 49160 | tf_op jit(solution)/shard_map/ppermute | solution.py:28
  348.5 89.1 %collective-permute-start.13 = (bf16[1,64,128]{2,1,0:T(8,128)(2,1)S(1)}, bf16[1,64,128]{2,1,0:T(8,128)(2,1)S(1)}, u32[]{:S(2)}, u32[]{:S(2)}) collective-permute-start(bf16[1,64,128]{2,1,0:T(8,128)(2,1)S(1)} %get-tuple-element.26), channel_id=1, source_target_pairs={{8,0},{16,8},{24,16},{32,24},{40,32},{48,40},{56,48},{64,56},{72,6... | collective-permute-start | bytes 49160 | tf_op jit(solution)/shard_map/ppermute | solution.py:30
  434.7 8.3 %collective-permute-start.6 = (bf16[6,64,1]{2,1,0:T(8,128)(2,1)S(1)}, bf16[6,64,1]{2,1,0:T(8,128)(2,1)S(1)}, u32[]{:S(2)}, u32[]{:S(2)}) collective-permute-start(bf16[6,64,1]{2,1,0:T(8,128)(2,1)S(1)} %get-tuple-element.20), channel_id=1, source_target_pairs={{0,1},{1,2},{2,3},{3,4},{4,5},{5,6},{6,7},{8,9},{9,10},{10,11},{11... | collective-permute-start | bytes 2312 | tf_op jit(solution)/shard_map/ppermute | solution.py:28
  436.3 6.8 collective-permute-start.7
  437.8 7.1 collective-permute-start.14
  441.8 7.1 %collective-permute-start.15 = (bf16[6,64,1]{2,1,0:T(8,128)(2,1)S(1)}, bf16[6,64,1]{2,1,0:T(8,128)(2,1)S(1)}, u32[]{:S(2)}, u32[]{:S(2)}) collective-permute-start(bf16[6,64,1]{2,1,0:T(8,128)(2,1)S(1)} %get-tuple-element.13), channel_id=1, source_target_pairs={{1,0},{2,1},{3,2},{4,3},{5,4},{6,5},{7,6},{9,8},{10,9},{11,10},{12... | collective-permute-start | bytes 2312 | tf_op jit(solution)/shard_map/ppermute | solution.py:30
Sparse Core Ops, SparseCore 0:
  10.8 85.3 all-reduce.3
  120.8 109.8 all-gather.1
  275.7 35.7 reduce-scatter.1
  450.5 250.8 all-reduce.5
